TPU v7x, 512 devices: a whole 4x8x8 slice. The times are simulated.
512 devices in a mesh: dp: 32 (over y, x), seq: 16 (over z, core).
Axes of the slice: x: 4, y: 8, z: 8, core: 2. Of those that a mesh axis runs over, the one named last changes fastest.
Arguments:
- queries: bfloat16 [32, 2048, 2048], P('dp', 'seq'), may hold values from -6 to 6
- keys_in: bfloat16 [32, 2048, 2048], P('dp', 'seq'), may hold values from -6 to 6
- values_in: bfloat16 [32, 2048, 2048], P('dp', 'seq'), may hold values from -6 to 6
- grad_out: bfloat16 [32, 2048, 2048], P('dp', 'seq'), may hold values from -6 to 6
- feat_w: bfloat16 [2, 16, 128, 128], replicated, may hold values from -0.5 to 0.5
Outputs:
- grad_queries: bfloat16 [32, 2048, 2048], P('dp', 'seq')
- grad_keys: bfloat16 [32, 2048, 2048], P('dp', 'seq')
- grad_values: bfloat16 [32, 2048, 2048], P('dp', 'seq')
- grad_feat: float32 [4096, 128], P('dp')
All inputs are finite; a program needn't handle non-finite values.
Results may differ from a plain program's by a relative error of at most 0.0064.
Values sent between devices are 32-bit elements; how exact they have to be, the bound alone decides.
A program may use at most 128 MiB of HBM per device.

v0:
```python
import math

import jax
import jax.numpy as jnp
from jax import lax
from jax.sharding import PartitionSpec as P


def carried_in(value, axis, join, neutral, backward):
    count, mine = (lax.axis_size(axis), lax.axis_index(axis))
    pieces = lax.all_gather(value, axis)
    if backward:
        pieces = pieces[::-1]
        mine = count - 1 - mine
    running = jnp.full_like(value, 0) + jnp.asarray(neutral, value.dtype)

    def lap(position, running):
        longer = join(running, pieces[position])
        return jnp.where(position < mine, longer, running)

    return lax.fori_loop(0, count - 1, lap, running)


def add_one(earlier, later):
    return earlier + later


def body(queries, keys_in, values_in, grad_out, feat_w):
    seq_count = lax.axis_size("seq")
    rep_count = lax.axis_size("dp")
    rows = queries.shape[1]
    heads = feat_w.shape[1]
    hsize = feat_w.shape[2]
    scale = 1.0 / math.sqrt(hsize * rows * seq_count)
    gscale = 1.0 / math.sqrt(rows * seq_count * rep_count)
    shape = (rows, heads, hsize)
    q_heads = queries[0].reshape(shape)
    k_heads = keys_in[0].reshape(shape)
    v_heads = values_in[0].reshape(shape)
    g_heads = grad_out[0].reshape(shape)
    f32 = jnp.float32
    bf16 = jnp.bfloat16
    feat_q = jnp.einsum("tha,hab->thb", q_heads, feat_w[0], preferred_element_type=f32).astype(bf16)
    feat_k = jnp.einsum("tha,hab->thb", k_heads, feat_w[1], preferred_element_type=f32).astype(bf16)
    sterm = jnp.einsum("tha,thb->hab", feat_k, v_heads, preferred_element_type=f32)
    gterm = jnp.einsum("tha,thb->hab", feat_q, g_heads, preferred_element_type=f32)
    zeros = jnp.zeros(sterm.shape, f32)
    prefix = carried_in(sterm, "seq", add_one, zeros, False)
    suffix = carried_in(gterm, "seq", add_one, zeros, True)
    causal = jnp.tril(jnp.ones((rows, rows), dtype=bool))
    p_mat = jnp.where(
        causal, scale * jnp.einsum("tha,sha->hts", feat_q, feat_k, preferred_element_type=f32), 0.0
    ).astype(bf16)
    q_mat = jnp.where(
        causal,
        scale * jnp.einsum("tha,sha->hts", g_heads, v_heads, preferred_element_type=f32),
        0.0,
    ).astype(bf16)
    state_b = prefix.astype(bf16)
    grad_b = suffix.astype(bf16)
    d_featq = (
        scale * jnp.einsum("thb,hab->tha", g_heads, state_b, preferred_element_type=f32)
        + jnp.einsum("hts,sha->tha", q_mat, feat_k, preferred_element_type=f32)
    ).astype(bf16)
    d_featk = (
        scale * jnp.einsum("thb,hab->tha", v_heads, grad_b, preferred_element_type=f32)
        + jnp.einsum("hts,tha->sha", q_mat, feat_q, preferred_element_type=f32)
    ).astype(bf16)
    d_values = (
        scale * jnp.einsum("tha,hab->thb", feat_k, grad_b, preferred_element_type=f32)
        + jnp.einsum("hts,thb->shb", p_mat, g_heads, preferred_element_type=f32)
    ).astype(bf16)
    d_queries = jnp.einsum("thb,hab->tha", d_featq, feat_w[0], preferred_element_type=f32).astype(
        bf16
    )
    d_keys = jnp.einsum("thb,hab->tha", d_featk, feat_w[1], preferred_element_type=f32).astype(bf16)
    wgrad_q = jnp.einsum("tha,thb->hab", q_heads, d_featq, preferred_element_type=f32)
    wgrad_k = jnp.einsum("tha,thb->hab", k_heads, d_featk, preferred_element_type=f32)
    local_grad = jnp.stack([wgrad_q, wgrad_k]).reshape(2 * heads * hsize, hsize)
    seq_total = lax.psum(local_grad, "seq")
    owned = lax.psum_scatter(seq_total, "dp", scatter_dimension=0, tiled=True)
    flat = (1, rows, heads * hsize)
    return (d_queries.reshape(flat), d_keys.reshape(flat), d_values.reshape(flat), owned * gscale)


def solution(mesh):
    return jax.shard_map(
        body,
        mesh=mesh,
        in_specs=(
            P("dp", "seq", None),
            P("dp", "seq", None),
            P("dp", "seq", None),
            P("dp", "seq", None),
            P(),
        ),
        out_specs=(P("dp", "seq", None), P("dp", "seq", None), P("dp", "seq", None), P("dp", None)),
        check_vma=False,
    )
```

profile of v0, /device:TPU:1, one launch (start us, length us, event | category | flops | bytes accessed | tf_op | source)
XLA Modules:
  0.0 593.4 jit_solution(17331871863249463423)
XLA Ops:
  7.2 1.3 copy.64
  8.5 1.3 copy.67
  9.9 1.6 fusion.11
  11.5 1.3 fusion.27
  12.8 0.0 all-gather.7.cloned.1.call-start
  12.9 1.3 copy.65
  14.2 1.3 copy.66
  15.5 1.6 fusion.12
  17.1 1.5 fusion.33
  18.6 0.0 reduce-scatter.2.cloned.1.call-start
  18.7 2.4 fusion.5
  21.1 96.6 %all-gather.5.cloned.1.call-done = f32[256,128,128]{2,1,0:T(8,128)} async-done(((f32[16,128,128]{2,1,0:T(8,128)}), f32[256,128,128]{2,1,0:T(8,128)}) %all-gather.5.cloned.1.call-update) | async-done | bytes 16777232 | tf_op jit(solution)/shard_map/all_gather | solution.py:11
  117.7 24.4 %while.28 = (s32[]{:T(128)}, f32[16,128,128]{2,1,0:T(8,128)S(1)}, s32[]{:T(128)}, f32[16,16,128,128]{3,2,1,0:T(8,128)}, s32[]{:T(128)}, /*index=5*/s32[]{:T(128)}) while((s32[]{:T(128)}, f32[16,128,128]{2,1,0:T(8,128)S(1)}, s32[]{:T(128)}, f32[16,16,128,128]{3,2,1,0:T(8,128)}, s32[]{:T(128)}, /*index=5*/s32[]{:T(128)}) %tuple.79), condition=%wide.region_1.2_spmd.clone, body=%wide.region_0.1_spmd.clone.sunk | while | flops 786436 | bytes 3145821 | solution.py:21
  117.7 1.6 add_select_fusion.4
  119.3 1.6 add_select_fusion.4
  120.9 1.6 add_select_fusion.4
  122.6 1.6 add_select_fusion.4
  124.2 1.6 add_select_fusion.4
  125.8 1.6 add_select_fusion.4
  127.4 1.6 add_select_fusion.4
  129.0 1.6 add_select_fusion.4
  130.6 1.7 add_select_fusion.4
  132.4 1.6 add_select_fusion.4
  134.0 1.6 add_select_fusion.4
  135.6 1.6 add_select_fusion.4
  137.2 1.6 add_select_fusion.4
  138.8 1.7 add_select_fusion.4
  140.5 1.6 add_select_fusion.4
  142.1 0.3 convolution_multiply_fusion.4
  142.4 1.5 fusion.10
  144.0 2.5 convolution_bitcast_fusion.2
  146.5 70.1 %all-gather.7.cloned.1.call-done = f32[256,128,128]{2,1,0:T(8,128)} async-done(((f32[16,128,128]{2,1,0:T(8,128)}), f32[256,128,128]{2,1,0:T(8,128)}) %all-gather.7.cloned.1.call-update) | async-done | bytes 16777232 | tf_op jit(solution)/shard_map/all_gather | solution.py:11
  216.6 11.6 %rev.3 = f32[16,16,128,128]{3,2,1,0:T(8,128)} reverse(f32[16,16,128,128]{3,2,1,0:T(8,128)} %bitcast.81), dimensions={0} | reverse | bytes 33554432 | tf_op jit(solution)/shard_map/rev | solution.py:13
  228.3 24.2 %while.29 = (s32[]{:T(128)}, f32[16,128,128]{2,1,0:T(8,128)S(1)}, s32[]{:T(128)}, f32[16,16,128,128]{3,2,1,0:T(8,128)}, s32[]{:T(128)}, /*index=5*/s32[]{:T(128)}) while((s32[]{:T(128)}, f32[16,128,128]{2,1,0:T(8,128)S(1)}, s32[]{:T(128)}, f32[16,16,128,128]{3,2,1,0:T(8,128)}, s32[]{:T(128)}, /*index=5*/s32[]{:T(128)}) %tuple.68), condition=%wide.region_3.4_spmd.clone, body=%wide.region_2.3_spmd.clone.sunk | while | flops 786436 | bytes 3145821 | solution.py:21
  228.3 1.6 add_select_fusion.5
  229.9 1.6 add_select_fusion.5
  231.6 1.6 add_select_fusion.5
  233.2 1.6 add_select_fusion.5
  234.8 1.6 add_select_fusion.5
  236.4 1.6 add_select_fusion.5
  238.0 1.6 add_select_fusion.5
  239.6 1.6 add_select_fusion.5
  241.2 1.6 add_select_fusion.5
  242.9 1.6 add_select_fusion.5
  244.5 1.6 add_select_fusion.5
  246.1 1.6 add_select_fusion.5
  247.7 1.6 add_select_fusion.5
  249.3 1.6 add_select_fusion.5
  250.9 1.6 add_select_fusion.5
  252.5 1.5 convolution_multiply_fusion.2
  254.1 1.3 fusion.9
  255.4 0.8 copy-done.2
  256.2 1.5 convolution_bitcast_fusion.1
  257.7 2.8 pad_maximum_fusion
  260.6 2.1 convolution_convert_fusion.1
  262.7 1.3 fusion.1
  264.0 1.7 fusion.8
  265.7 208.6 %reduce-scatter.2.cloned.1.call-done = f32[128,128]{1,0:T(8,128)} async-done(((f32[4096,128]{1,0:T(8,128)}), f32[128,128]{1,0:T(8,128)}) %reduce-scatter.2.cloned.1.call-update) | async-done | bytes 65552 | tf_op jit(solution)/shard_map/reduce_scatter | solution.py:81
  474.3 1.5 convolution_convert_fusion
  475.8 1.0 copy.54
  476.9 2.0 copy.52
  478.9 1.0 copy.53
  479.9 105.5 %all-reduce.2.cloned.1.call-done = f32[128,128]{1,0:T(8,128)} async-done(((f32[128,128]{1,0:T(8,128)}), f32[128,128]{1,0:T(8,128)}) %all-reduce.2.cloned.1.call-update) | async-done | bytes 65552 | tf_op jit(solution)/shard_map/psum | solution.py:80
  585.4 1.5 broadcast_multiply_fusion
  (20 shorter events, 0.2 us)
Async XLA Ops:
  7.2 110.5 %all-gather.5.cloned.1.call-start = ((), (), s32[]{:S(2)}) async-start(), calls=%async_computation.1 | async-start | bytes 17825792 | tf_op jit(solution)/shard_map/all_gather | solution.py:11
  8.5 4.3 copy-start.3
  9.9 5.6 copy-start.4
  12.8 203.8 %all-gather.7.cloned.1.call-start = ((), (), s32[]{:S(2)}) async-start(), calls=%async_computation.2 | async-start | bytes 17825792 | tf_op jit(solution)/shard_map/all_gather | solution.py:11
  15.5 3.2 copy-start.5
  17.1 1.6 copy-start
  18.6 455.7 %reduce-scatter.2.cloned.1.call-start = ((), (), s32[]{:S(2)}) async-start(), calls=%async_computation.3 | async-start | bytes 2162688 | tf_op jit(solution)/shard_map/reduce_scatter | solution.py:81
  228.3 25.8 %copy-start.1 = (bf16[128,16,128]{0,2,1:T(8,128)(2,1)S(1)}, bf16[128,16,128]{0,2,1:T(8,128)(2,1)}, u32[]{:S(2)}) copy-start(bf16[128,16,128]{0,2,1:T(8,128)(2,1)} %copy-done) | copy-start | bytes 1572868
  255.4 0.8 copy-start.2
  260.5 324.9 %all-reduce.2.cloned.1.call-start = ((), (), s32[]{:S(2)}) async-start(), calls=%async_computation.4 | async-start | bytes 131072 | tf_op jit(solution)/shard_map/psum | solution.py:80
Sparse Core Ops, SparseCore 0:
  12.9 104.7 all-gather.4
  119.8 96.7 all-gather.6
  260.6 213.6 reduce-scatter.1
  476.6 108.7 all-reduce.1
where the time goes:
time: 595 us; the launch traced here: 593 us
  waiting for transfers between devices  481 us (81%)
  other arithmetic  52.2 us (9%)
  matrix products  23.7 us (4%)
  local copies, waits for them, and re-layouts  21.8 us (4%)
  between operations  14 us (2%)
    reduce_scatter x1, waiting for transfers between devices, body(): owned = lax.psum_scatter(seq_total, 'dp', scatter_dimension=0, tiled=True)  209 us
    all_gather x2, waiting for transfers between devices, carried_in(): pieces = lax.all_gather(value, axis)  167 us
    psum x1, waiting for transfers between devices, body(): seq_total = lax.psum(local_grad, 'seq')  105 us
    select_n x30, other arithmetic, lap(): return jnp.where(position < mine, longer, running)  48 us
  transfers between devices with their start and end apart: 4, of which 4 were waited for; matrix products, arithmetic and copies ran while one was open for 8% of the time, Pallas kernels for 0%

commit v1 on v0

v1 whole, which is shorter than its diff:
```python
import functools
import math

import jax
import jax.numpy as jnp
from jax import lax
from jax.experimental import pallas as pl
from jax.experimental.pallas import tpu as pltpu
from jax.sharding import PartitionSpec as P

MESH = pl.DeviceIdType.MESH
F32 = jnp.float32
BF16 = jnp.bfloat16


def dot(a, b, ca, cb):
    return lax.dot_general(a, b, (((ca,), (cb,)), ((), ())), preferred_element_type=F32)


def remote(src, dst, send, recv, where):
    return pltpu.make_async_remote_copy(
        src_ref=src, dst_ref=dst, send_sem=send, recv_sem=recv, device_id=where, device_id_type=MESH
    )


def attention_kernel(
    scale,
    chips,
    q_ref,
    k_ref,
    v_ref,
    g_ref,
    w_ref,
    dq_ref,
    dk_ref,
    dv_ref,
    wg_ref,
    fq_ref,
    fk_ref,
    terms,
    mate,
    chain,
    onward,
    states,
    lent,
    mate_send,
    mate_recv,
    chain_send,
    chain_recv,
    lent_send,
    lent_recv,
):
    heads = w_ref.shape[1]
    size = w_ref.shape[2]
    rows = q_ref.shape[0]
    count = 2 * chips
    seq = lax.axis_index("seq")
    z = seq // 2
    core = seq % 2
    own = 1 - core
    partner = seq + 1 - 2 * core
    nxt = (seq + 4 * core - 2 + count) % count
    prv = (seq - 4 * core + 2 + count) % count
    hop = z * core + (chips - 1 - z) * (1 - core)
    first = hop == 0
    last = hop == chips - 1

    barrier = pltpu.get_barrier_semaphore()
    for other in (partner, nxt, prv):
        pl.semaphore_signal(barrier, inc=1, device_id={"seq": other}, device_id_type=MESH)

    def cols(h):
        return pl.ds(pl.multiple_of(h * size, size), size)

    def mate_copy(h):
        return remote(
            terms.at[core, h], mate.at[h], mate_send.at[h], mate_recv.at[h], {"seq": partner}
        )

    def chain_copy(h):
        return remote(
            onward.at[h], chain.at[h], chain_send.at[h], chain_recv.at[h], {"seq": nxt}
        )

    def lent_copy(h):
        return remote(chain.at[h], lent.at[h], lent_send.at[h], lent_recv.at[h], {"seq": partner})

    def features(h):
        c = cols(h)
        fq = dot(q_ref[:, c], w_ref[0, h], 1, 0).astype(BF16)
        fk = dot(k_ref[:, c], w_ref[1, h], 1, 0).astype(BF16)
        fq_ref[:, c] = fq
        fk_ref[:, c] = fk
        terms[0, h] = dot(fk, v_ref[:, c], 0, 0)
        terms[1, h] = dot(fq, g_ref[:, c], 0, 0)

    features(0)
    features(1)
    pl.semaphore_wait(barrier, 3)

    @pl.when(first)
    def _():
        chain[...] = jnp.zeros_like(chain)

    mate_copy(0).start()
    mate_copy(1).start()

    def start(i, carry):
        features(2 * i)
        features(2 * i + 1)
        mate_copy(2 * i).start()
        mate_copy(2 * i + 1).start()
        return carry

    lax.fori_loop(1, heads // 2, start, 0)

    causal = lax.broadcasted_iota(jnp.int32, (rows, rows), 0) >= lax.broadcasted_iota(
        jnp.int32, (rows, rows), 1
    )

    def masked(a, b):
        return jnp.where(causal, scale * dot(a, b, 1, 1), 0.0).astype(BF16)

    def query_side(h, state):
        c = cols(h)
        g = g_ref[:, c]
        qm = masked(g, v_ref[:, c])
        dfq = (scale * dot(g, state, 1, 1) + dot(qm, fk_ref[:, c], 1, 0)).astype(BF16)
        dq_ref[:, c] = dot(dfq, w_ref[0, h], 1, 1).astype(BF16)
        wg_ref[:, h] = dot(q_ref[:, c], dfq, 0, 0).reshape(rows // 8, 8, size)

    def key_side(h, state):
        c = cols(h)
        g = g_ref[:, c]
        v = v_ref[:, c]
        fq = fq_ref[:, c]
        fk = fk_ref[:, c]
        qm = masked(g, v)
        pm = masked(fq, fk)
        dfk = (scale * dot(v, state, 1, 1) + dot(qm, fq, 0, 0)).astype(BF16)
        dv_ref[:, c] = (scale * dot(fk, state, 1, 0) + dot(pm, g, 0, 0)).astype(BF16)
        dk_ref[:, c] = dot(dfk, w_ref[1, h], 1, 1).astype(BF16)
        wg_ref[:, heads + h] = dot(k_ref[:, c], dfk, 0, 0).reshape(rows // 8, 8, size)

    def own_pair(i):
        @pl.when(core == 1)
        def _():
            for h in (2 * i, 2 * i + 1):
                query_side(h, states[h])

        @pl.when(core == 0)
        def _():
            for h in (2 * i, 2 * i + 1):
                key_side(h, states[h])

    def lent_pair(i):
        lent_copy(2 * i).wait_recv()
        lent_copy(2 * i + 1).wait_recv()

        @pl.when(core == 0)
        def _():
            for h in (2 * i, 2 * i + 1):
                query_side(h, lent[h].astype(BF16))

        @pl.when(core == 1)
        def _():
            for h in (2 * i, 2 * i + 1):
                key_side(h, lent[h].astype(BF16))

    early = jnp.clip(4 * hop - 2 * chips + 2, 0, heads // 2)

    def ahead(i, carry):
        @pl.when(i < early)
        def _():
            lent_pair(i)

        return carry

    lax.fori_loop(0, heads // 2, ahead, 0)

    def link(h):
        mate_copy(h).wait_recv()

        @pl.when(jnp.logical_not(first))
        def _():
            chain_copy(h).wait_recv()

        mine = chain[h] + mate[h]

        @pl.when(jnp.logical_not(last))
        def _():
            onward[h] = mine + terms[own, h]
            chain_copy(h).start()

        lent_copy(h).start()
        states[h] = mine.astype(BF16)

    def links(i, carry):
        link(2 * i)
        link(2 * i + 1)

        @pl.when(last)
        def _():
            own_pair(i)

        return carry

    lax.fori_loop(0, heads // 2, links, 0)

    def behind(i, carry):
        @pl.when(jnp.logical_not(last))
        def _():
            own_pair(i)

        return carry

    lax.fori_loop(0, heads // 2, behind, 0)

    def rest(i, carry):
        @pl.when(i >= early)
        def _():
            lent_pair(i)

        return carry

    lax.fori_loop(0, heads // 2, rest, 0)

    def drain(h, carry):
        mate_copy(h).wait_send()
        lent_copy(h).wait_send()

        @pl.when(jnp.logical_not(last))
        def _():
            chain_copy(h).wait_send()

        return carry

    lax.fori_loop(0, heads, drain, 0)


def attention(queries, keys_in, values_in, grad_out, feat_w, scale, chips):
    rows, width = queries.shape
    heads, size = feat_w.shape[1:3]
    vmem = pl.BlockSpec(memory_space=pltpu.VMEM)
    rowed = jax.ShapeDtypeStruct((rows, width), BF16)
    state = pltpu.VMEM((heads, size, size), F32)
    sem = pltpu.SemaphoreType.DMA((heads,))
    return pl.pallas_call(
        functools.partial(attention_kernel, scale, chips),
        out_shape=[
            rowed,
            rowed,
            rowed,
            jax.ShapeDtypeStruct((size // 8, 2 * heads, 8, size), F32),
        ],
        in_specs=[vmem] * 5,
        out_specs=[vmem] * 4,
        scratch_shapes=[
            pltpu.VMEM((rows, width), BF16),
            pltpu.VMEM((rows, width), BF16),
            pltpu.VMEM((2, heads, size, size), F32),
            state,
            state,
            state,
            pltpu.VMEM((heads, size, size), BF16),
            state,
            sem,
            sem,
            sem,
            sem,
            sem,
            sem,
        ],
        compiler_params=pltpu.CompilerParams(collective_id=0, has_side_effects=True),
        name="attention",
    )(queries, keys_in, values_in, grad_out, feat_w)


def reduce_kernel(
    nz,
    ny,
    nx,
    w_ref,
    out_ref,
    mate,
    up,
    up_in,
    down,
    down_in,
    mine,
    y_in,
    part,
    x_in,
    whole,
    mate_send,
    mate_recv,
    up_send,
    up_recv,
    down_send,
    down_recv,
    y_send,
    y_recv,
    x_send,
    x_recv,
    z_send,
    z_recv,
    last_send,
    last_recv,
):
    seq = lax.axis_index("seq")
    dp = lax.axis_index("dp")
    z = seq // 2
    core = seq % 2
    y = dp // nx
    x = dp % nx
    partner = {"seq": seq + 1 - 2 * core}

    def at_z(j):
        return {"seq": ((z + j + nz) % nz) * 2 + core}

    def at_y(j):
        return {"dp": ((y + j) % ny) * nx + x}

    def at_x(j):
        return {"dp": y * nx + (x + j) % nx}

    barrier = pltpu.get_barrier_semaphore()
    peers = [partner]
    peers += [at_z(j) for j in range(1, nz)]
    peers += [at_y(j) for j in range(1, ny)]
    peers += [at_x(j) for j in range(1, nx)]
    for peer in peers:
        pl.semaphore_signal(barrier, inc=1, device_id=peer, device_id_type=MESH)
    pl.semaphore_wait(barrier, len(peers))

    ups = nz // 2
    downs = nz - 1 - ups
    blocks = w_ref.shape[1]
    half = blocks // 2

    order = []
    for j in range(ups):
        order.append(ups - j)
        if j < downs:
            order.append(nz - (downs - j))
    order.append(0)
    mates = {}
    for j in order:
        t = (z + j) % nz
        mates[j] = remote(
            w_ref.at[(1 - core) * nz + t], mate.at[j], mate_send.at[j], mate_recv.at[j], partner
        )
        mates[j].start()

    waited = set()

    def local(j, span):
        if j not in waited:
            waited.add(j)
            mates[j].wait_recv()
        return w_ref[core * nz + (z + j) % nz, span] + mate[j, span]

    sends = []
    up_copies = {}
    down_copies = {}
    for step in range(ups):
        for part_no in range(2):
            span = pl.ds(part_no * half, half)
            for name, steps, buf, inbox, ss, rs, copies in (
                ("up", ups, up, up_in, up_send, up_recv, up_copies),
                ("down", downs, down, down_in, down_send, down_recv, down_copies),
            ):
                if step >= steps:
                    continue
                j = ups - step if name == "up" else nz - (downs - step)
                value = local(j, span)
                if step:
                    copies[step - 1, part_no].wait_recv()
                    value = value + inbox[step - 1, span]
                buf[step, span] = value
                copy = remote(
                    buf.at[step, span],
                    inbox.at[step, span],
                    ss.at[step, part_no],
                    rs.at[step, part_no],
                    at_z(1 if name == "up" else -1),
                )
                copy.start()
                copies[step, part_no] = copy
                sends.append(copy)

    y_copies = []
    for part_no in range(2):
        span = pl.ds(part_no * half, half)
        value = local(0, span)
        up_copies[ups - 1, part_no].wait_recv()
        down_copies[downs - 1, part_no].wait_recv()
        mine[span] = value + up_in[ups - 1, span] + down_in[downs - 1, span]

    for j in range(1, ny):
        there = (y + j) % ny
        copy = remote(
            mine.at[pl.ds(there * nx, nx)], y_in.at[j], y_send.at[j], y_recv.at[j], at_y(j)
        )
        copy.start()
        y_copies.append(copy)
    total = mine[pl.ds(y * nx, nx)]
    for j in range(1, ny):
        y_copies[j - 1].wait_recv()
        total = total + y_in[j]
    part[...] = total
    x_copies = []
    for j in range(1, nx):
        copy = remote(part.at[(x + j) % nx], x_in.at[j], x_send.at[j], x_recv.at[j], at_x(j))
        copy.start()
        x_copies.append(copy)
    total = part[x]
    for j in range(1, nx):
        x_copies[j - 1].wait_recv()
        total = total + x_in[j]
    whole[core, z] = total

    z_copies = []
    for j in range(1, nz):
        copy = remote(
            whole.at[core, z], whole.at[core, z], z_send.at[j], z_recv.at[j], at_z(j)
        )
        copy.start()
        z_copies.append(copy)
    for j in range(1, nz):
        z_copies[j - 1].wait_recv()
    copy = remote(whole.at[core], whole.at[core], last_send, last_recv, partner)
    copy.start()
    copy.wait_recv()
    out_ref[...] = whole[...]

    sends += y_copies + x_copies + z_copies + [copy] + [mates[j] for j in order]
    for copy in sends:
        copy.wait_send()


def reduce_grad(pieces, nz, ny, nx):
    groups, blocks, sub, size = pieces.shape
    vmem = pl.BlockSpec(memory_space=pltpu.VMEM)
    dma = pltpu.SemaphoreType.DMA
    ups = nz // 2
    downs = nz - 1 - ups
    return pl.pallas_call(
        functools.partial(reduce_kernel, nz, ny, nx),
        out_shape=jax.ShapeDtypeStruct((2, nz, sub, size), F32),
        in_specs=[vmem],
        out_specs=vmem,
        scratch_shapes=[
            pltpu.VMEM((nz, blocks, sub, size), F32),
            pltpu.VMEM((ups, blocks, sub, size), F32),
            pltpu.VMEM((ups, blocks, sub, size), F32),
            pltpu.VMEM((downs, blocks, sub, size), F32),
            pltpu.VMEM((downs, blocks, sub, size), F32),
            pltpu.VMEM((blocks, sub, size), F32),
            pltpu.VMEM((ny, nx, sub, size), F32),
            pltpu.VMEM((nx, sub, size), F32),
            pltpu.VMEM((nx, sub, size), F32),
            pltpu.VMEM((2, nz, sub, size), F32),
            dma((nz,)),
            dma((nz,)),
            dma((ups, 2)),
            dma((ups, 2)),
            dma((downs, 2)),
            dma((downs, 2)),
            dma((ny,)),
            dma((ny,)),
            dma((nx,)),
            dma((nx,)),
            dma((nz,)),
            dma((nz,)),
            dma,
            dma,
        ],
        compiler_params=pltpu.CompilerParams(collective_id=1, has_side_effects=True),
        name="reduce_grad",
    )(pieces)


def body(queries, keys_in, values_in, grad_out, feat_w):
    seq_count = lax.axis_size("seq")
    rep_count = lax.axis_size("dp")
    rows = queries.shape[1]
    hsize = feat_w.shape[2]
    scale = 1.0 / math.sqrt(hsize * rows * seq_count)
    gscale = 1.0 / math.sqrt(rows * seq_count * rep_count)
    nz = seq_count // 2
    nx = 4
    ny = rep_count // nx
    d_queries, d_keys, d_values, pieces = attention(
        queries[0], keys_in[0], values_in[0], grad_out[0], feat_w, scale, nz
    )
    owned = reduce_grad(pieces, nz, ny, nx).reshape(hsize, hsize)
    return (d_queries[None], d_keys[None], d_values[None], owned * gscale)


def solution(mesh):
    return jax.shard_map(
        body,
        mesh=mesh,
        in_specs=(
            P("dp", "seq", None),
            P("dp", "seq", None),
            P("dp", "seq", None),
            P("dp", "seq", None),
            P(),
        ),
        out_specs=(P("dp", "seq", None), P("dp", "seq", None), P("dp", "seq", None), P("dp", None)),
        check_vma=False,
    )
```

time: 595 us -> 101 us (0.17)
  waiting for transfers between devices: 481 us -> 0 us
  Pallas kernels: 0 us -> 96.6 us
  other arithmetic: 52.2 us -> 1.47 us
  matrix products: 23.7 us -> 0 us
  local copies, waits for them, and re-layouts: 21.8 us -> 2.39 us
  between operations: 14 us -> 0.67 us
    reduce_scatter x1 -> x0, waiting for transfers between devices: 209 us -> none  [body(): owned = lax.psum_scatter(seq_total, 'dp', scatter_dimension=0, tiled=True)]
    all_gather x2 -> x0, waiting for transfers between devices: 167 us -> none  [carried_in(): pieces = lax.all_gather(value, axis)]
    psum x1 -> x0, waiting for transfers between devices: 105 us -> none  [body(): seq_total = lax.psum(local_grad, 'seq')]
    pallas_call x0 -> x2, Pallas kernels: none -> 96.6 us  [the longest x1 54.4 us: attention(): pl.pallas_call(functools.partial(attention_kernel, scale, chips), out_sha...]
    select_n x30 -> x0, other arithmetic: 48 us -> none  [lap(): return jnp.where(position < mine, longer, running)]
    dot_general x15 -> x0, matrix products: 23.7 us -> none  [the longest x1 2.51 us: body(): jnp.einsum('tha,thb->hab', q_heads, d_featq, preferred_element_type=f32)]
    rev x1 -> x0, local copies, waits for them, and re-layouts: 11.6 us -> none  [carried_in(): pieces = pieces[::-1]]
  transfers between devices with their start and end apart: 4 -> 0, of which waited for: 4 -> 0; matrix products, arithmetic and copies ran while one was open for 8% -> 0% of each run, Pallas kernels for 0% -> 0%
where the time goes in v1:
time: 101 us
  Pallas kernels  96.6 us (96%)
  local copies, waits for them, and re-layouts  2.39 us (2%)
  other arithmetic  1.47 us (1%)
    pallas_call x1, Pallas kernels, attention(): pl.pallas_call(functools.partial(attention_kernel, scale, chips), out_sha...  54.4 us
    pallas_call x1, Pallas kernels, reduce_grad(): pl.pallas_call(functools.partial(reduce_kernel, nz, ny, nx), out_shape=ja...  42.3 us
    unnamed x9, local copies, waits for them, and re-layouts  2.39 us

profile of v1, /device:TPU:1, one launch (start us, length us, event | category | flops | bytes accessed | tf_op | source)
XLA Modules:
  0.0 101.2 jit_solution(10185831406809504085)
XLA Ops:
  0.6 54.4 %attention.1 = (bf16[128,2048]{1,0:T(8,128)(2,1)}, bf16[128,2048]{1,0:T(8,128)(2,1)}, bf16[128,2048]{1,0:T(8,128)(2,1)}, f32[16,32,8,128]{3,2,1,0:T(8,128)}) custom-call(bf16[128,2048]{1,0:T(8,128)(2,1)} %bitcast.11, bf16[128,2048]{1,0:T(8,128)(2,1)} %bitcast.12, bf16[128,2048]{1,0:T(8,128)(2,1)} %bitcast.13, bf16[128,2048]{1,0:T(8,128)(2,1)} %bitcast.14, ...), custom_call_target="tpu_custom_call" | custom-call | tf_op jit(solution)/shard_map/attention/pallas_call | solution.py:248
  55.0 0.0 copy-start.2
  55.0 0.0 copy-start.1
  55.0 0.0 copy-start
  55.0 42.3 %reduce_grad.1 = f32[2,8,8,128]{3,2,1,0:T(8,128)} custom-call(f32[16,32,8,128]{3,2,1,0:T(8,128)} %get-tuple-element.11.w_ref), custom_call_target="tpu_custom_call" | custom-call | tf_op jit(solution)/shard_map/reduce_grad/pallas_call | solution.py:448
  97.3 1.5 %broadcast_multiply_fusion = f32[2,8,8,128]{3,2,1,0:T(8,128)} fusion(f32[2,8,8,128]{3,2,1,0:T(8,128)} %reduce_grad.1), kind=kLoop, calls=%fused_computation | loop fusion | flops 16384 | bytes 131072 | tf_op jit(solution)/shard_map/mul | solution.py:498
  98.8 0.0 copy-done.2
  98.8 0.8 copy.12
  99.6 0.0 copy-done.1
  99.6 0.8 copy.13
  100.4 0.0 copy-done
  100.4 0.8 copy.14
Async XLA Ops:
  55.0 43.8 %copy-start.2 = (bf16[128,2048]{1,0:T(8,128)(2,1)S(1)}, bf16[128,2048]{1,0:T(8,128)(2,1)}, u32[]{:S(2)}) copy-start(bf16[128,2048]{1,0:T(8,128)(2,1)} %get-tuple-element.8) | copy-start | bytes 1572868
  55.0 44.6 %copy-start.1 = (bf16[128,2048]{1,0:T(8,128)(2,1)S(1)}, bf16[128,2048]{1,0:T(8,128)(2,1)}, u32[]{:S(2)}) copy-start(bf16[128,2048]{1,0:T(8,128)(2,1)} %get-tuple-element.9) | copy-start | bytes 1572868
  55.0 45.4 %copy-start = (bf16[128,2048]{1,0:T(8,128)(2,1)S(1)}, bf16[128,2048]{1,0:T(8,128)(2,1)}, u32[]{:S(2)}) copy-start(bf16[128,2048]{1,0:T(8,128)(2,1)} %get-tuple-element.10) | copy-start | bytes 1572868

commit v2 on v1

v2 whole, which is shorter than its diff:
```python
import functools
import math

import jax
import jax.numpy as jnp
from jax import lax
from jax.experimental import pallas as pl
from jax.experimental.pallas import tpu as pltpu
from jax.sharding import PartitionSpec as P

MESH = pl.DeviceIdType.MESH
F32 = jnp.float32
BF16 = jnp.bfloat16


def dot(a, b, ca, cb):
    return lax.dot_general(a, b, (((ca,), (cb,)), ((), ())), preferred_element_type=F32)


def remote(src, dst, send, recv, where):
    return pltpu.make_async_remote_copy(
        src_ref=src, dst_ref=dst, send_sem=send, recv_sem=recv, device_id=where, device_id_type=MESH
    )


def attention_kernel(
    scale,
    chips,
    ny,
    nx,
    q_ref,
    k_ref,
    v_ref,
    g_ref,
    w_ref,
    dq_ref,
    dk_ref,
    dv_ref,
    out_ref,
    fq_ref,
    fk_ref,
    terms,
    mate,
    chain,
    onward,
    states,
    lent,
    mate_send,
    mate_recv,
    chain_send,
    chain_recv,
    lent_send,
    lent_recv,
    wg_ref,
    pair,
    up,
    up_in,
    down,
    down_in,
    mine_ref,
    y_in,
    part,
    x_in,
    whole,
    pair_send,
    pair_recv,
    up_send,
    up_recv,
    down_send,
    down_recv,
    y_send,
    y_recv,
    x_send,
    x_recv,
    z_send,
    z_recv,
    last_send,
    last_recv,
):
    heads = w_ref.shape[1]
    size = w_ref.shape[2]
    rows = q_ref.shape[0]
    count = 2 * chips
    seq = lax.axis_index("seq")
    z = seq // 2
    core = seq % 2
    own = 1 - core
    partner = seq + 1 - 2 * core
    nxt = (seq + 4 * core - 2 + count) % count
    hop = z * core + (chips - 1 - z) * (1 - core)
    first = hop == 0
    last = hop == chips - 1

    dp = lax.axis_index("dp")
    y = dp // nx
    x = dp % nx

    def at_z(j):
        return {"seq": ((z + j + chips) % chips) * 2 + core}

    def at_y(j):
        return {"dp": ((y + j) % ny) * nx + x}

    def at_x(j):
        return {"dp": y * nx + (x + j) % nx}

    barrier = pltpu.get_barrier_semaphore()
    peers = [{"seq": partner}]
    peers += [at_z(j) for j in range(1, chips)]
    peers += [at_y(j) for j in range(1, ny)]
    peers += [at_x(j) for j in range(1, nx)]
    for peer in peers:
        pl.semaphore_signal(barrier, inc=1, device_id=peer, device_id_type=MESH)

    def cols(h):
        return pl.ds(pl.multiple_of(h * size, size), size)

    def mate_copy(h):
        return remote(
            terms.at[core, h], mate.at[h], mate_send.at[h], mate_recv.at[h], {"seq": partner}
        )

    def chain_copy(h):
        return remote(
            onward.at[h], chain.at[h], chain_send.at[h], chain_recv.at[h], {"seq": nxt}
        )

    def lent_copy(h):
        return remote(chain.at[h], lent.at[h], lent_send.at[h], lent_recv.at[h], {"seq": partner})

    def features(h):
        c = cols(h)
        fq = dot(q_ref[:, c], w_ref[0, h], 1, 0).astype(BF16)
        fk = dot(k_ref[:, c], w_ref[1, h], 1, 0).astype(BF16)
        fq_ref[:, c] = fq
        fk_ref[:, c] = fk
        terms[0, h] = dot(fk, v_ref[:, c], 0, 0)
        terms[1, h] = dot(fq, g_ref[:, c], 0, 0)

    features(0)
    features(1)
    pl.semaphore_wait(barrier, len(peers))

    @pl.when(first)
    def _():
        chain[...] = jnp.zeros_like(chain)

    mate_copy(0).start()
    mate_copy(1).start()

    def start(i, carry):
        features(2 * i)
        features(2 * i + 1)
        mate_copy(2 * i).start()
        mate_copy(2 * i + 1).start()
        return carry

    lax.fori_loop(1, heads // 2, start, 0)

    causal = lax.broadcasted_iota(jnp.int32, (rows, rows), 0) >= lax.broadcasted_iota(
        jnp.int32, (rows, rows), 1
    )

    def masked(a, b):
        return jnp.where(causal, scale * dot(a, b, 1, 1), 0.0).astype(BF16)

    def block(h, side):
        return (h // nx) * (2 * nx) + side * nx + h % nx

    def pair_copy(d):
        return remote(
            wg_ref.at[pl.ds((1 - core) * chips, chips), d],
            pair.at[:, d],
            pair_send.at[d],
            pair_recv.at[d],
            {"seq": partner},
        )

    def query_side(h, state):
        c = cols(h)
        g = g_ref[:, c]
        qm = masked(g, v_ref[:, c])
        dfq = (scale * dot(g, state, 1, 1) + dot(qm, fk_ref[:, c], 1, 0)).astype(BF16)
        dq_ref[:, c] = dot(dfq, w_ref[0, h], 1, 1).astype(BF16)
        wg_ref[:, block(h, 0)] = dot(q_ref[:, c], dfq, 0, 0).reshape(rows // 8, 8, size)

    def key_side(h, state):
        c = cols(h)
        g = g_ref[:, c]
        v = v_ref[:, c]
        fq = fq_ref[:, c]
        fk = fk_ref[:, c]
        qm = masked(g, v)
        pm = masked(fq, fk)
        dfk = (scale * dot(v, state, 1, 1) + dot(qm, fq, 0, 0)).astype(BF16)
        dv_ref[:, c] = (scale * dot(fk, state, 1, 0) + dot(pm, g, 0, 0)).astype(BF16)
        dk_ref[:, c] = dot(dfk, w_ref[1, h], 1, 1).astype(BF16)
        wg_ref[:, block(h, 1)] = dot(k_ref[:, c], dfk, 0, 0).reshape(rows // 8, 8, size)

    def own_pair(i):
        @pl.when(core == 1)
        def _():
            for h in (2 * i, 2 * i + 1):
                query_side(h, states[h])

        @pl.when(core == 0)
        def _():
            for h in (2 * i, 2 * i + 1):
                key_side(h, states[h])

        for h in (2 * i, 2 * i + 1):
            pair_copy(block(h, 1 - core)).start()

    def lent_pair(i):
        lent_copy(2 * i).wait_recv()
        lent_copy(2 * i + 1).wait_recv()

        @pl.when(core == 0)
        def _():
            for h in (2 * i, 2 * i + 1):
                query_side(h, lent[h].astype(BF16))

        @pl.when(core == 1)
        def _():
            for h in (2 * i, 2 * i + 1):
                key_side(h, lent[h].astype(BF16))

        for h in (2 * i, 2 * i + 1):
            pair_copy(block(h, core)).start()

    early = jnp.clip(4 * hop - 2 * chips + 2, 0, heads // 2)

    def ahead(i, carry):
        @pl.when(i < early)
        def _():
            lent_pair(i)

        return carry

    lax.fori_loop(0, heads // 2, ahead, 0)

    def link(h):
        mate_copy(h).wait_recv()

        @pl.when(jnp.logical_not(first))
        def _():
            chain_copy(h).wait_recv()

        mine = chain[h] + mate[h]

        @pl.when(jnp.logical_not(last))
        def _():
            onward[h] = mine + terms[own, h]
            chain_copy(h).start()

        lent_copy(h).start()
        states[h] = mine.astype(BF16)

    def links(i, carry):
        link(2 * i)
        link(2 * i + 1)

        @pl.when(last)
        def _():
            own_pair(i)

        return carry

    lax.fori_loop(0, heads // 2, links, 0)

    def gradients(i):
        @pl.when(jnp.logical_not(last))
        def _():
            own_pair(i)

        @pl.when(i >= early)
        def _():
            lent_pair(i)

    groups = heads // nx
    group = 2 * nx
    pairs = heads // 2 // groups
    ups = chips // 2
    downs = chips - 1 - ups

    def span_of(n):
        return pl.ds(pl.multiple_of(n * group, group), group)

    def local(j, span):
        t = (z + j) % chips
        return wg_ref[core * chips + t, span] + pair[t, span]

    def up_copy(step, n):
        span = span_of(n)
        return remote(
            up.at[step, span], up_in.at[step, span], up_send.at[step, n], up_recv.at[step, n], at_z(1)
        )

    def down_copy(step, n):
        span = span_of(n)
        return remote(
            down.at[step, span],
            down_in.at[step, span],
            down_send.at[step, n],
            down_recv.at[step, n],
            at_z(-1),
        )

    def advance(step, n):
        span = span_of(n)
        if step == 0:

            def arrived(d, carry):
                pair_copy(n * group + d).wait_recv()
                return carry

            lax.fori_loop(0, group, arrived, 0)
        if step < ups:
            value = local(ups - step, span)
            if step:
                up_copy(step - 1, n).wait_recv()
                value = value + up_in[step - 1, span]
            up[step, span] = value
            up_copy(step, n).start()
        if step < downs:
            value = local(chips - (downs - step), span)
            if step:
                down_copy(step - 1, n).wait_recv()
                value = value + down_in[step - 1, span]
            down[step, span] = value
            down_copy(step, n).start()
        if step == ups:
            up_copy(ups - 1, n).wait_recv()
            down_copy(downs - 1, n).wait_recv()
            mine_ref[span] = local(0, span) + up_in[ups - 1, span] + down_in[downs - 1, span]
            for side in range(2):
                there = side * groups + n

                @pl.when(there != y)
                def _():
                    y_copy((there - y + ny) % ny).start()

    def y_span(there):
        return pl.ds((there % groups) * group + (there // groups) * nx, nx)

    def y_copy(j):
        return remote(
            mine_ref.at[y_span((y + j) % ny)], y_in.at[j], y_send.at[j], y_recv.at[j], at_y(j)
        )

    def slot(s, carry):
        @pl.when(s < groups)
        def _():
            for p in range(pairs):
                gradients(pairs * s + p)

        for step in range(ups + 1):

            @pl.when((s >= step) & (s < step + groups))
            def _():
                advance(step, s - step)

        return carry

    lax.fori_loop(0, groups + ups, slot, 0)

    total = mine_ref[y_span(y)]
    for j in range(1, ny):
        y_copy(j).wait_recv()
        total = total + y_in[j]
    part[...] = total
    x_copies = []
    for j in range(1, nx):
        copy = remote(part.at[(x + j) % nx], x_in.at[j], x_send.at[j], x_recv.at[j], at_x(j))
        copy.start()
        x_copies.append(copy)
    total = part[x]
    for j in range(1, nx):
        x_copies[j - 1].wait_recv()
        total = total + x_in[j]
    whole[core, z] = total

    z_copies = []
    for j in range(1, chips):
        copy = remote(whole.at[core, z], whole.at[core, z], z_send.at[j], z_recv.at[j], at_z(j))
        copy.start()
        z_copies.append(copy)
    for copy in z_copies:
        copy.wait_recv()
    final = remote(whole.at[core], whole.at[core], last_send, last_recv, {"seq": partner})
    final.start()

    def drain(h, carry):
        mate_copy(h).wait_send()
        lent_copy(h).wait_send()

        @pl.when(jnp.logical_not(last))
        def _():
            chain_copy(h).wait_send()

        return carry

    lax.fori_loop(0, heads, drain, 0)

    def drain_blocks(d, carry):
        pair_copy(d).wait_send()
        return carry

    lax.fori_loop(0, 2 * heads, drain_blocks, 0)

    def drain_groups(n, carry):
        for step in range(ups):
            up_copy(step, n).wait_send()
        for step in range(downs):
            down_copy(step, n).wait_send()
        return carry

    lax.fori_loop(0, groups, drain_groups, 0)
    for j in range(1, ny):
        y_copy(j).wait_send()
    for copy in x_copies + z_copies:
        copy.wait_send()
    final.wait()
    out_ref[...] = whole[...]


def attention(queries, keys_in, values_in, grad_out, feat_w, scale, chips, ny, nx):
    rows, width = queries.shape
    heads, size = feat_w.shape[1:3]
    vmem = pl.BlockSpec(memory_space=pltpu.VMEM)
    rowed = jax.ShapeDtypeStruct((rows, width), BF16)
    state = pltpu.VMEM((heads, size, size), F32)
    dma = pltpu.SemaphoreType.DMA
    ups = chips // 2
    downs = chips - 1 - ups
    blocks = 2 * heads
    sub = size // (2 * chips)

    def pieces(*lead):
        return pltpu.VMEM((*lead, sub, size), F32)

    return pl.pallas_call(
        functools.partial(attention_kernel, scale, chips, ny, nx),
        out_shape=[rowed] * 3 + [jax.ShapeDtypeStruct((2, chips, sub, size), F32)],
        in_specs=[vmem] * 5,
        out_specs=[vmem] * 4,
        scratch_shapes=[
            pltpu.VMEM((rows, width), BF16),
            pltpu.VMEM((rows, width), BF16),
            pltpu.VMEM((2, heads, size, size), F32),
            state,
            state,
            state,
            pltpu.VMEM((heads, size, size), BF16),
            state,
        ]
        + [dma((heads,))] * 6
        + [
            pieces(2 * chips, blocks),
            pieces(chips, blocks),
            pieces(ups, blocks),
            pieces(ups, blocks),
            pieces(downs, blocks),
            pieces(downs, blocks),
            pieces(blocks),
            pieces(ny, nx),
            pieces(nx),
            pieces(nx),
            pieces(2, chips),
        ]
        + [dma((blocks,))] * 2
        + [dma((ups, heads // nx))] * 2
        + [dma((downs, heads // nx))] * 2
        + [dma((ny,))] * 2
        + [dma((nx,))] * 2
        + [dma((chips,))] * 2
        + [dma] * 2,
        compiler_params=pltpu.CompilerParams(collective_id=0, has_side_effects=True),
        name="attention",
    )(queries, keys_in, values_in, grad_out, feat_w)


def finish_kernel(gscale, a_ref, b_ref, c_ref, d_ref, oa_ref, ob_ref, oc_ref, od_ref):
    oa_ref[...] = a_ref[...]
    ob_ref[...] = b_ref[...]
    oc_ref[...] = c_ref[...]
    od_ref[...] = d_ref[...] * gscale


def finish(arrays, gscale, steps=2):
    specs = [
        pl.BlockSpec((a.shape[0] // steps, a.shape[1]), lambda i: (i, 0)) for a in arrays
    ]
    return pl.pallas_call(
        functools.partial(finish_kernel, gscale),
        grid=(steps,),
        out_shape=[jax.ShapeDtypeStruct(a.shape, a.dtype) for a in arrays],
        in_specs=specs,
        out_specs=specs,
        name="finish",
    )(*arrays)


def body(queries, keys_in, values_in, grad_out, feat_w):
    seq_count = lax.axis_size("seq")
    rep_count = lax.axis_size("dp")
    rows = queries.shape[1]
    hsize = feat_w.shape[2]
    scale = 1.0 / math.sqrt(hsize * rows * seq_count)
    gscale = 1.0 / math.sqrt(rows * seq_count * rep_count)
    nz = seq_count // 2
    nx = 4
    ny = rep_count // nx
    d_queries, d_keys, d_values, owned = attention(
        queries[0], keys_in[0], values_in[0], grad_out[0], feat_w, scale, nz, ny, nx
    )
    results = finish((d_queries, d_keys, d_values, owned.reshape(hsize, hsize)), gscale)
    return (results[0][None], results[1][None], results[2][None], results[3])


def solution(mesh):
    return jax.shard_map(
        body,
        mesh=mesh,
        in_specs=(
            P("dp", "seq", None),
            P("dp", "seq", None),
            P("dp", "seq", None),
            P("dp", "seq", None),
            P(),
        ),
        out_specs=(P("dp", "seq", None), P("dp", "seq", None), P("dp", "seq", None), P("dp", None)),
        check_vma=False,
    )
```

time: 101 us -> 96.5 us (0.955); the launches traced: 101 us -> 95.2 us
  local copies, waits for them, and re-layouts: 2.39 us -> 0 us
  Pallas kernels: 96.6 us -> 94.5 us
  other arithmetic: 1.47 us -> 0 us
    unnamed x9 -> x0, local copies, waits for them, and re-layouts: 2.39 us -> none
    pallas_call x2, Pallas kernels: 96.6 us -> 94.5 us  [the longest x1 92.2 us: attention(): pl.pallas_call(functools.partial(attention_kernel, scale, chips, ny, nx),...]
    mul x1 -> x0, other arithmetic: 1.47 us -> none  [body(): return (d_queries[None], d_keys[None], d_values[None], owned * gscale)]
where the time goes in v2:
time: 96.5 us; the launch traced here: 95.2 us
  Pallas kernels  94.5 us (98%)
    pallas_call x1, Pallas kernels, attention(): pl.pallas_call(functools.partial(attention_kernel, scale, chips, ny, nx),...  92.2 us
    pallas_call x1, Pallas kernels, finish(): pl.pallas_call(functools.partial(finish_kernel, gscale), grid=(steps,), o...  2.33 us

profile of v2, /device:TPU:1, one launch (start us, length us, event | category | flops | bytes accessed | tf_op | source)
XLA Modules:
  0.0 95.2 jit_solution(3029151484793739369)
XLA Ops:
  0.6 92.2 %attention.1 = (bf16[128,2048]{1,0:T(8,128)(2,1)}, bf16[128,2048]{1,0:T(8,128)(2,1)}, bf16[128,2048]{1,0:T(8,128)(2,1)}, f32[2,8,8,128]{3,2,1,0:T(8,128)}) custom-call(bf16[128,2048]{1,0:T(8,128)(2,1)} %bitcast.8, bf16[128,2048]{1,0:T(8,128)(2,1)} %bitcast.9, bf16[128,2048]{1,0:T(8,128)(2,1)} %bitcast.10, bf16[128,2048]{1,0:T(8,128)(2,1)} %bitcast.11, ...), custom_call_target="tpu_custom_call" | custom-call | tf_op jit(solution)/shard_map/attention/pallas_call | solution.py:442
  92.8 2.3 %finish.1 = (bf16[128,2048]{1,0:T(8,128)(2,1)}, bf16[128,2048]{1,0:T(8,128)(2,1)}, bf16[128,2048]{1,0:T(8,128)(2,1)}, f32[128,128]{1,0:T(8,128)}) custom-call(bf16[128,2048]{1,0:T(8,128)(2,1)} %get-tuple-element.12.a_ref, bf16[128,2048]{1,0:T(8,128)(2,1)} %get-tuple-element.13.b_ref, bf16[128,2048]{1,0:T(8,128)(2,1)} %get-tuple-element.14.c_ref, ...), custom_call_target="tpu_custom_call" | custom-call | tf_op jit(solution)/shard_map/finish/pallas_call | solution.py:494

commit v3 on v2

--- a/solution.py
+++ b/solution.py
@@ -8,6 +8,7 @@
 from jax.experimental.pallas import tpu as pltpu
 from jax.sharding import PartitionSpec as P
 
+SPLIT = 4
 MESH = pl.DeviceIdType.MESH
 F32 = jnp.float32
 BF16 = jnp.bfloat16
@@ -44,6 +45,7 @@
     chain,
     onward,
     states,
+    lend,
     lent,
     mate_send,
     mate_recv,
@@ -74,8 +76,6 @@
     x_recv,
     z_send,
     z_recv,
-    last_send,
-    last_recv,
 ):
     heads = w_ref.shape[1]
     size = w_ref.shape[2]
@@ -84,10 +84,11 @@
     seq = lax.axis_index("seq")
     z = seq // 2
     core = seq % 2
-    own = 1 - core
+    role = 1 - core
+    own = 1 - role
     partner = seq + 1 - 2 * core
-    nxt = (seq + 4 * core - 2 + count) % count
-    hop = z * core + (chips - 1 - z) * (1 - core)
+    nxt = (seq + 4 * role - 2 + count) % count
+    hop = z * role + (chips - 1 - z) * (1 - role)
     first = hop == 0
     last = hop == chips - 1
 
@@ -98,6 +99,9 @@
     def at_z(j):
         return {"seq": ((z + j + chips) % chips) * 2 + core}
 
+    def across(j):
+        return {"seq": ((z + j + chips) % chips) * 2 + 1 - core}
+
     def at_y(j):
         return {"dp": ((y + j) % ny) * nx + x}
 
@@ -105,7 +109,7 @@
         return {"dp": y * nx + (x + j) % nx}
 
     barrier = pltpu.get_barrier_semaphore()
-    peers = [{"seq": partner}]
+    peers = [across(j) for j in range(chips)]
     peers += [at_z(j) for j in range(1, chips)]
     peers += [at_y(j) for j in range(1, ny)]
     peers += [at_x(j) for j in range(1, nx)]
@@ -117,16 +121,24 @@
 
     def mate_copy(h):
         return remote(
-            terms.at[core, h], mate.at[h], mate_send.at[h], mate_recv.at[h], {"seq": partner}
+            terms.at[role, h], mate.at[h], mate_send.at[h], mate_recv.at[h], {"seq": partner}
         )
 
-    def chain_copy(h):
+    def chain_span(r):
+        return pl.ds(r * (size // SPLIT), size // SPLIT)
+
+    def chain_copy(h, r):
+        n = h * SPLIT + r
         return remote(
-            onward.at[h], chain.at[h], chain_send.at[h], chain_recv.at[h], {"seq": nxt}
+            onward.at[h, chain_span(r)],
+            chain.at[h, chain_span(r)],
+            chain_send.at[n],
+            chain_recv.at[n],
+            {"seq": nxt},
         )
 
     def lent_copy(h):
-        return remote(chain.at[h], lent.at[h], lent_send.at[h], lent_recv.at[h], {"seq": partner})
+        return remote(lend.at[h], lent.at[h], lent_send.at[h], lent_recv.at[h], {"seq": partner})
 
     def features(h):
         c = cols(h)
@@ -148,11 +160,42 @@
     mate_copy(0).start()
     mate_copy(1).start()
 
+    def link(h):
+        mate_copy(h).wait_recv()
+
+        for r in range(SPLIT):
+            span = chain_span(r)
+
+            @pl.when(jnp.logical_not(first))
+            def _():
+                chain_copy(h, r).wait_recv()
+
+            mine = chain[h, span]
+            both = mine + terms[own, h, span]
+
+            @pl.when(jnp.logical_not(last))
+            def _():
+                onward[h, span] = both + mate[h, span]
+                chain_copy(h, r).start()
+
+            lend[h, span] = both
+            states[h, span] = mine.astype(BF16)
+
+        lent_copy(h).start()
+
+    lag = 3
+
     def start(i, carry):
         features(2 * i)
         features(2 * i + 1)
         mate_copy(2 * i).start()
         mate_copy(2 * i + 1).start()
+
+        @pl.when(first & (i >= lag))
+        def _():
+            link(2 * (i - lag))
+            link(2 * (i - lag) + 1)
+
         return carry
 
     lax.fori_loop(1, heads // 2, start, 0)
@@ -198,35 +241,35 @@
         wg_ref[:, block(h, 1)] = dot(k_ref[:, c], dfk, 0, 0).reshape(rows // 8, 8, size)
 
     def own_pair(i):
-        @pl.when(core == 1)
+        @pl.when(role == 1)
         def _():
             for h in (2 * i, 2 * i + 1):
                 query_side(h, states[h])
 
-        @pl.when(core == 0)
+        @pl.when(role == 0)
         def _():
             for h in (2 * i, 2 * i + 1):
                 key_side(h, states[h])
 
         for h in (2 * i, 2 * i + 1):
-            pair_copy(block(h, 1 - core)).start()
+            pair_copy(block(h, 1 - role)).start()
 
     def lent_pair(i):
         lent_copy(2 * i).wait_recv()
         lent_copy(2 * i + 1).wait_recv()
 
-        @pl.when(core == 0)
+        @pl.when(role == 0)
         def _():
             for h in (2 * i, 2 * i + 1):
                 query_side(h, lent[h].astype(BF16))
 
-        @pl.when(core == 1)
+        @pl.when(role == 1)
         def _():
             for h in (2 * i, 2 * i + 1):
                 key_side(h, lent[h].astype(BF16))
 
         for h in (2 * i, 2 * i + 1):
-            pair_copy(block(h, core)).start()
+            pair_copy(block(h, role)).start()
 
     early = jnp.clip(4 * hop - 2 * chips + 2, 0, heads // 2)
 
@@ -239,26 +282,11 @@
 
     lax.fori_loop(0, heads // 2, ahead, 0)
 
-    def link(h):
-        mate_copy(h).wait_recv()
-
-        @pl.when(jnp.logical_not(first))
-        def _():
-            chain_copy(h).wait_recv()
-
-        mine = chain[h] + mate[h]
-
-        @pl.when(jnp.logical_not(last))
-        def _():
-            onward[h] = mine + terms[own, h]
-            chain_copy(h).start()
-
-        lent_copy(h).start()
-        states[h] = mine.astype(BF16)
-
     def links(i, carry):
-        link(2 * i)
-        link(2 * i + 1)
+        @pl.when(jnp.logical_not(first) | (i >= heads // 2 - lag))
+        def _():
+            link(2 * i)
+            link(2 * i + 1)
 
         @pl.when(last)
         def _():
@@ -381,14 +409,15 @@
     whole[core, z] = total
 
     z_copies = []
-    for j in range(1, chips):
-        copy = remote(whole.at[core, z], whole.at[core, z], z_send.at[j], z_recv.at[j], at_z(j))
-        copy.start()
-        z_copies.append(copy)
-    for copy in z_copies:
-        copy.wait_recv()
-    final = remote(whole.at[core], whole.at[core], last_send, last_recv, {"seq": partner})
-    final.start()
+    for j in range(chips // 2, -chips // 2, -1):
+        for n, peer in enumerate((at_z, across)):
+            if j or n:
+                n = (j % chips) * 2 + n
+                copy = remote(
+                    whole.at[core, z], whole.at[core, z], z_send.at[n], z_recv.at[n], peer(j)
+                )
+                copy.start()
+                z_copies.append(copy)
 
     def drain(h, carry):
         mate_copy(h).wait_send()
@@ -396,7 +425,8 @@
 
         @pl.when(jnp.logical_not(last))
         def _():
-            chain_copy(h).wait_send()
+            for r in range(SPLIT):
+                chain_copy(h, r).wait_send()
 
         return carry
 
@@ -420,7 +450,8 @@
         y_copy(j).wait_send()
     for copy in x_copies + z_copies:
         copy.wait_send()
-    final.wait()
+    for copy in z_copies:
+        copy.wait_recv()
     out_ref[...] = whole[...]
 
 
@@ -453,8 +484,11 @@
             state,
             pltpu.VMEM((heads, size, size), BF16),
             state,
+            state,
         ]
-        + [dma((heads,))] * 6
+        + [dma((heads,))] * 2
+        + [dma((heads * SPLIT,))] * 2
+        + [dma((heads,))] * 2
         + [
             pieces(2 * chips, blocks),
             pieces(chips, blocks),
@@ -473,8 +507,7 @@
         + [dma((downs, heads // nx))] * 2
         + [dma((ny,))] * 2
         + [dma((nx,))] * 2
-        + [dma((chips,))] * 2
-        + [dma] * 2,
+        + [dma((2 * chips,))] * 2,
         compiler_params=pltpu.CompilerParams(collective_id=0, has_side_effects=True),
         name="attention",
     )(queries, keys_in, values_in, grad_out, feat_w)

time: 96.5 us -> 90.1 us (0.934)
  Pallas kernels: 94.5 us -> 87.9 us
    pallas_call x1, Pallas kernels: 92.2 us -> 85.6 us  [attention(): pl.pallas_call(functools.partial(attention_kernel, scale, chips, ny, nx),...]
where the time goes in v3:
time: 90.1 us; the launch traced here: 88.6 us
  Pallas kernels  87.9 us (98%)
    pallas_call x1, Pallas kernels, attention(): pl.pallas_call(functools.partial(attention_kernel, scale, chips, ny, nx),...  85.6 us
    pallas_call x1, Pallas kernels, finish(): pl.pallas_call(functools.partial(finish_kernel, gscale), grid=(steps,), o...  2.33 us

profile of v3, /device:TPU:1, one launch (start us, length us, event | category | flops | bytes accessed | tf_op | source)
XLA Modules:
  0.0 88.6 jit_solution(11631469021374562058)
XLA Ops:
  0.6 85.6 %attention.1 = (bf16[128,2048]{1,0:T(8,128)(2,1)}, bf16[128,2048]{1,0:T(8,128)(2,1)}, bf16[128,2048]{1,0:T(8,128)(2,1)}, f32[2,8,8,128]{3,2,1,0:T(8,128)}) custom-call(bf16[128,2048]{1,0:T(8,128)(2,1)} %bitcast.8, bf16[128,2048]{1,0:T(8,128)(2,1)} %bitcast.9, bf16[128,2048]{1,0:T(8,128)(2,1)} %bitcast.10, bf16[128,2048]{1,0:T(8,128)(2,1)} %bitcast.11, ...), custom_call_target="tpu_custom_call" | custom-call | tf_op jit(solution)/shard_map/attention/pallas_call | solution.py:473
  86.2 2.3 %finish.1 = (bf16[128,2048]{1,0:T(8,128)(2,1)}, bf16[128,2048]{1,0:T(8,128)(2,1)}, bf16[128,2048]{1,0:T(8,128)(2,1)}, f32[128,128]{1,0:T(8,128)}) custom-call(bf16[128,2048]{1,0:T(8,128)(2,1)} %get-tuple-element.12.a_ref, bf16[128,2048]{1,0:T(8,128)(2,1)} %get-tuple-element.13.b_ref, bf16[128,2048]{1,0:T(8,128)(2,1)} %get-tuple-element.14.c_ref, ...), custom_call_target="tpu_custom_call" | custom-call | tf_op jit(solution)/shard_map/finish/pallas_call | solution.py:527
